TPU v7x, 512 devices: a whole 4x4x16 slice. The times are simulated.
512 devices in a mesh: loop: 64 (over z, x_hi, core), narrow: 8 (over x_lo, y).
Axes of the slice: x: 4 (x_hi: 2, x_lo: 2; x = x_hi * 2 + x_lo), y: 4, z: 16, core: 2. Of those that a mesh axis runs over, the one named last changes fastest.
Arguments:
- tokens: bfloat16 [1024, 8192], P('loop', 'narrow'), may hold values from -6 to 6
- gate_weight: bfloat16 [8192, 28672], P('narrow', 'loop'), may hold values from -0.0625 to 0.0625
- up_weight: bfloat16 [8192, 28672], P('narrow', 'loop'), may hold values from -0.0625 to 0.0625
- down_weight: bfloat16 [28672, 8192], P('loop', 'narrow'), may hold values from -0.03125 to 0.03125
Outputs:
- mixed: bfloat16 [1024, 8192], P('loop', 'narrow')
All inputs are finite; a program needn't handle non-finite values.
Results may differ from a plain program's by a relative error of at most 0.0049.
Values may be sent and summed in bfloat16 or wider, within the bound.
No kernel may reach another device: no remote copies, remote signals or barrier semaphores. Data moves between devices by JAX's collectives and lax.ppermute only.
A program may use at most 64 MiB of HBM per device.

v0:
```python
import jax
import jax.numpy as jnp
from jax import lax
from jax.sharding import Mesh, PartitionSpec as P

AXES = ("zh", "zl", "xh", "core", "xl", "y")
Z = ("zh", "zl")
NARROW = ("xl", "y")
SWAP = [(0, 1), (1, 0)]


def f32dot(a, b):
    return jnp.dot(a, b, preferred_element_type=jnp.float32)


def shards(tokens, gate_weight, up_weight, down_weight):
    gate_other = lax.ppermute(gate_weight, "core", SWAP)
    up_other = lax.ppermute(up_weight, "core", SWAP)
    down_other = lax.ppermute(down_weight, "core", SWAP)
    rows = lax.all_gather(tokens, Z, axis=0, tiled=True)
    near = lax.all_to_all(jnp.broadcast_to(rows, (2, *rows.shape)), "xh", 0, 0)
    rows = near.reshape(-1, tokens.shape[1])
    n_rows = rows.shape[0]
    gates = jnp.concatenate((gate_weight, gate_other), axis=1)
    ups = jnp.concatenate((up_weight, up_other), axis=1)
    width = gates.shape[1]
    partial = jnp.concatenate(
        (f32dot(rows, gates).astype(jnp.bfloat16), f32dot(rows, ups).astype(jnp.bfloat16)), axis=1
    )
    partial = partial.reshape(8, n_rows // 8, 2 * width)
    parts = lax.all_to_all(partial, NARROW, 0, 0)
    totals = jnp.sum(parts.astype(jnp.float32), axis=0)
    hidden = (jax.nn.silu(totals[:, :width]) * totals[:, width:]).astype(jnp.bfloat16)
    hidden = lax.all_to_all(jnp.broadcast_to(hidden, (8, *hidden.shape)), NARROW, 0, 0)
    hidden = hidden.reshape(n_rows, width)
    downs = jnp.concatenate((down_weight, down_other), axis=0)
    mixed = f32dot(hidden, downs).astype(jnp.bfloat16)
    mixed = mixed.reshape(2, 4, 4, 16, -1)
    mixed = mixed.transpose(2, 0, 1, 3, 4).reshape(8, 64, -1)
    mixed = lax.all_to_all(mixed, ("zl", "xh"), 0, 0)
    mixed = jnp.sum(mixed.astype(jnp.float32), axis=0).astype(jnp.bfloat16)
    mixed = lax.all_to_all(mixed.reshape(4, 16, -1), "zh", 0, 0)
    return jnp.sum(mixed.astype(jnp.float32), axis=0).astype(jnp.bfloat16)


def solution(mesh):
    fine = Mesh(mesh.devices.reshape(4, 4, 2, 2, 2, 4), AXES)
    loop, narrow = (("zh", "zl", "xh", "core"), NARROW)
    return jax.shard_map(
        shards,
        mesh=fine,
        in_specs=(P(loop, narrow), P(narrow, loop), P(narrow, loop), P(loop, narrow)),
        out_specs=P(loop, narrow),
        check_vma=False,
    )
```

profile of v0, /device:TPU:2, one launch (start us, length us, event | category | flops | bytes accessed | tf_op | source)
XLA Modules:
  0.0 147.9 jit_solution(17875800447940083722)
XLA Ops:
  0.0 1.9 %collective-permute-start = (bf16[1024,448]{0,1:T(8,128)(2,1)}, bf16[1024,448]{0,1:T(8,128)(2,1)S(1)}, u32[]{:S(2)}, u32[]{:S(2)}) collective-permute-start(bf16[1024,448]{0,1:T(8,128)(2,1)} %param.5), channel_id=1, source_target_pairs={{0,8},{8,0},{1,9},{9,1},{2,10},{10,2},{3,11},{11,3},{4,12},{12,4},... | collective-permute-start | bytes 2752520 | tf_op jit(solution)/shard_map/ppermute | solution.py:17
  1.9 2.4 %collective-permute-start.1 = (bf16[1024,448]{0,1:T(8,128)(2,1)}, bf16[1024,448]{0,1:T(8,128)(2,1)S(1)}, u32[]{:S(2)}, u32[]{:S(2)}) collective-permute-start(bf16[1024,448]{0,1:T(8,128)(2,1)} %param.6), channel_id=1, source_target_pairs={{0,8},{8,0},{1,9},{9,1},{2,10},{10,2},{3,11},{11,3},{4,12},{12,4},... | collective-permute-start | bytes 2752520 | tf_op jit(solution)/shard_map/ppermute | solution.py:18
  4.3 38.8 %all_gather.3 = bf16[256,1024]{1,0:T(8,128)(2,1)S(1)} all-gather(bf16[16,1024]{1,0:T(8,128)(2,1)} %param.4), channel_id=1, replica_groups=mesh['zh'=4,'zl'=4,'xh'=2,'core'=2,'xl'=2,'y'=4] {'zh','zl'}, dimensions={0}, use_global_device_ids=true | all-gather | bytes 557056 | tf_op jit(solution)/shard_map/all_gather | solution.py:20
  43.2 0.0 copy-start
  43.2 0.1 broadcast_in_dim.6
  43.3 14.2 %all_to_all.25 = bf16[2,256,1024]{2,1,0:T(8,128)(2,1)S(1)} all-to-all(bf16[2,256,1024]{2,1,0:T(8,128)(2,1)S(1)} %broadcast_in_dim.6), channel_id=1, replica_groups=mesh['zh'=4,'zl'=4,'xh'=2,'core'=2,'xl'=2,'y'=4] {'xh'}, dimensions={0} | all-to-all | bytes 2097152 | tf_op jit(solution)/shard_map/all_to_all | solution.py:21
  57.5 0.0 collective-permute-done
  57.5 0.0 copy-done
  57.5 0.0 copy-start.1
  57.5 1.1 fusion.21
  58.7 0.0 collective-permute-done.1
  58.7 0.0 copy-done.1
  58.7 1.1 fusion.24
  59.8 0.1 pad_maximum_fusion
  60.0 2.5 %copy.7 = bf16[512,1792]{1,0:T(8,128)(2,1)} copy(bf16[512,1792]{0,1:T(8,128)(2,1)S(1)} %pad_maximum_fusion) | data formatting | bytes 3670016 | tf_op jit(solution)/shard_map/concatenate | solution.py:27
  62.4 0.0 copy-start.2
  62.4 6.1 %all-to-all-start.1 = ((bf16[8,64,1792]{2,1,0:T(8,128)(2,1)}), bf16[8,64,1792]{2,1,0:T(8,128)(2,1)S(1)}, u32[]{:S(2)}, u32[]{:S(2)}) async-start(bf16[8,64,1792]{2,1,0:T(8,128)(2,1)} %bitcast.3), calls=%async_computation.1 | async-start | bytes 3670016 | tf_op jit(solution)/shard_map/all_to_all | solution.py:31
  68.5 0.0 copy-done.2
  68.5 1.9 %collective-permute-start.2 = (bf16[448,1024]{1,0:T(8,128)(2,1)S(1)}, bf16[448,1024]{1,0:T(8,128)(2,1)}, u32[]{:S(2)}, u32[]{:S(2)}) collective-permute-start(bf16[448,1024]{1,0:T(8,128)(2,1)S(1)} %copy-done.2), channel_id=1, source_target_pairs={{0,8},{8,0},{1,9},{9,1},{2,10},{10,2},{3,11},{11,3},{4,12},{12,4},... | collective-permute-start | bytes 2752520 | tf_op jit(solution)/shard_map/ppermute | solution.py:19
  70.4 12.6 %all-to-all-done.1 = bf16[8,64,1792]{2,1,0:T(8,128)(2,1)S(1)} async-done(((bf16[8,64,1792]{2,1,0:T(8,128)(2,1)}), bf16[8,64,1792]{2,1,0:T(8,128)(2,1)S(1)}, u32[]{:S(2)}, u32[]{:S(2)}) %all-to-all-start.1) | async-done | bytes 1835040 | tf_op jit(solution)/shard_map/all_to_all | solution.py:31
  83.0 0.2 convert_reduce_fusion
  83.3 0.1 fusion.27
  83.3 1.0 broadcast_in_dim.7
  84.4 4.3 %all-to-all-start.2 = ((bf16[8,64,896]{2,1,0:T(8,128)(2,1)}), bf16[8,64,896]{2,1,0:T(8,128)(2,1)S(1)}, u32[]{:S(2)}, u32[]{:S(2)}) async-start(bf16[8,64,896]{2,1,0:T(8,128)(2,1)} %broadcast_in_dim.7), calls=%async_computation.2 | async-start | bytes 1835008 | tf_op jit(solution)/shard_map/all_to_all | solution.py:34
  88.7 0.0 collective-permute-done.2
  88.7 9.3 %all-to-all-done.2 = bf16[8,64,896]{2,1,0:T(8,128)(2,1)S(1)} async-done(((bf16[8,64,896]{2,1,0:T(8,128)(2,1)}), bf16[8,64,896]{2,1,0:T(8,128)(2,1)S(1)}, u32[]{:S(2)}, u32[]{:S(2)}) %all-to-all-start.2) | async-done | bytes 917536 | tf_op jit(solution)/shard_map/all_to_all | solution.py:34
  98.1 2.4 %fusion.12 = bf16[512,1024]{1,0:T(8,128)(2,1)S(1)} fusion(bf16[512,896]{1,0:T(8,128)(2,1)S(1)} %bitcast.19, bf16[448,1024]{1,0:T(8,128)(2,1)} %collective-permute-done.2, bf16[448,1024]{1,0:T(8,128)(2,1)S(1)} %copy-done.2), kind=kOutput, calls=%fused_computation.14 | convolution fusion | flops 943718400 | bytes 3801088 | tf_op jit(solution)/shard_map/dot_general | solution.py:13
  100.5 0.1 copy.8
  100.6 23.7 %all_to_all.26 = bf16[8,64,1024]{2,1,0:T(8,128)(2,1)S(1)} all-to-all(bf16[8,64,1024]{2,1,0:T(8,128)(2,1)S(1)} %bitcast.15), channel_id=1, replica_groups=mesh['zh'=4,'zl'=4,'xh'=2,'core'=2,'xl'=2,'y'=4] {'zl','xh'}, dimensions={0} | all-to-all | bytes 2097152 | tf_op jit(solution)/shard_map/all_to_all | solution.py:40
  124.3 0.2 reduce_sum.34
  124.5 22.8 %all_to_all.27 = bf16[4,16,1024]{2,1,0:T(8,128)(2,1)S(1)} all-to-all(bf16[4,16,1024]{2,1,0:T(8,128)(2,1)S(1)} %bitcast.20), channel_id=1, replica_groups=mesh['zh'=4,'zl'=4,'xh'=2,'core'=2,'xl'=2,'y'=4] {'zh'}, dimensions={0} | all-to-all | bytes 262144 | tf_op jit(solution)/shard_map/all_to_all | solution.py:42
  147.3 0.6 reduce_sum.35
Async XLA Ops:
  0.0 57.5 %collective-permute-start = (bf16[1024,448]{0,1:T(8,128)(2,1)}, bf16[1024,448]{0,1:T(8,128)(2,1)S(1)}, u32[]{:S(2)}, u32[]{:S(2)}) collective-permute-start(bf16[1024,448]{0,1:T(8,128)(2,1)} %param.5), channel_id=1, source_target_pairs={{0,8},{8,0},{1,9},{9,1},{2,10},{10,2},{3,11},{11,3},{4,12},{12,4},... | collective-permute-start | bytes 2752520 | tf_op jit(solution)/shard_map/ppermute | solution.py:17
  1.9 56.8 %collective-permute-start.1 = (bf16[1024,448]{0,1:T(8,128)(2,1)}, bf16[1024,448]{0,1:T(8,128)(2,1)S(1)}, u32[]{:S(2)}, u32[]{:S(2)}) collective-permute-start(bf16[1024,448]{0,1:T(8,128)(2,1)} %param.6), channel_id=1, source_target_pairs={{0,8},{8,0},{1,9},{9,1},{2,10},{10,2},{3,11},{11,3},{4,12},{12,4},... | collective-permute-start | bytes 2752520 | tf_op jit(solution)/shard_map/ppermute | solution.py:18
  43.2 14.4 %copy-start = (bf16[1024,448]{0,1:T(8,128)(2,1)S(1)}, bf16[1024,448]{0,1:T(8,128)(2,1)}, u32[]{:S(2)}) copy-start(bf16[1024,448]{0,1:T(8,128)(2,1)} %param.5) | copy-start | bytes 2752516
  57.5 1.2 copy-start.1
  62.4 6.1 %copy-start.2 = (bf16[448,1024]{1,0:T(8,128)(2,1)S(1)}, bf16[448,1024]{1,0:T(8,128)(2,1)}, u32[]{:S(2)}) copy-start(bf16[448,1024]{1,0:T(8,128)(2,1)} %param.7) | copy-start | bytes 2752516
  62.4 20.6 %all-to-all-start.1 = ((bf16[8,64,1792]{2,1,0:T(8,128)(2,1)}), bf16[8,64,1792]{2,1,0:T(8,128)(2,1)S(1)}, u32[]{:S(2)}, u32[]{:S(2)}) async-start(bf16[8,64,1792]{2,1,0:T(8,128)(2,1)} %bitcast.3), calls=%async_computation.1 | async-start | bytes 3670016 | tf_op jit(solution)/shard_map/all_to_all | solution.py:31
  68.5 20.2 %collective-permute-start.2 = (bf16[448,1024]{1,0:T(8,128)(2,1)S(1)}, bf16[448,1024]{1,0:T(8,128)(2,1)}, u32[]{:S(2)}, u32[]{:S(2)}) collective-permute-start(bf16[448,1024]{1,0:T(8,128)(2,1)S(1)} %copy-done.2), channel_id=1, source_target_pairs={{0,8},{8,0},{1,9},{9,1},{2,10},{10,2},{3,11},{11,3},{4,12},{12,4},... | collective-permute-start | bytes 2752520 | tf_op jit(solution)/shard_map/ppermute | solution.py:19
  84.4 13.7 %all-to-all-start.2 = ((bf16[8,64,896]{2,1,0:T(8,128)(2,1)}), bf16[8,64,896]{2,1,0:T(8,128)(2,1)S(1)}, u32[]{:S(2)}, u32[]{:S(2)}) async-start(bf16[8,64,896]{2,1,0:T(8,128)(2,1)} %broadcast_in_dim.7), calls=%async_computation.2 | async-start | bytes 1835008 | tf_op jit(solution)/shard_map/all_to_all | solution.py:34
where the time goes:
time: 148 us
  blocking collectives  99.5 us (67%)
  waiting for transfers between devices  21.9 us (15%)
  starting transfers between devices  16.6 us (11%)
  matrix products  4.72 us (3%)
  local copies, waits for them, and re-layouts  3.77 us (3%)
    all_gather x1, blocking collectives, shards(): rows = lax.all_gather(tokens, Z, axis=0, tiled=True)  38.8 us
    all_to_all x1, blocking collectives, shards(): mixed = lax.all_to_all(mixed, ('zl', 'xh'), 0, 0)  23.7 us
    all_to_all x1, blocking collectives, shards(): mixed = lax.all_to_all(mixed.reshape(4, 16, -1), 'zh', 0, 0)  22.8 us
    all_to_all x1, blocking collectives, shards(): near = lax.all_to_all(jnp.broadcast_to(rows, (2, *rows.shape)), 'xh', 0, 0)  14.2 us
    all_to_all x1, waiting for transfers between devices, shards(): parts = lax.all_to_all(partial, NARROW, 0, 0)  12.6 us
    all_to_all x1, waiting for transfers between devices, shards(): lax.all_to_all(jnp.broadcast_to(hidden, (8, *hidden.shape)), NARROW, 0, 0)  9.33 us
    all_to_all x1, starting transfers between devices, shards(): parts = lax.all_to_all(partial, NARROW, 0, 0)  6.06 us
    dot_general x3, matrix products, f32dot(): return jnp.dot(a, b, preferred_element_type=jnp.float32)  4.72 us
  transfers between devices with their start and end apart: 5, of which 2 were waited for; matrix products, arithmetic and copies ran while one was open for 2% of the time, Pallas kernels for 0%

commit v1 on v0

--- a/solution.py
+++ b/solution.py
@@ -17,7 +17,10 @@
     gate_other = lax.ppermute(gate_weight, "core", SWAP)
     up_other = lax.ppermute(up_weight, "core", SWAP)
     down_other = lax.ppermute(down_weight, "core", SWAP)
-    rows = lax.all_gather(tokens, Z, axis=0, tiled=True)
+    entries = []
+    for _ in range(lax.axis_size(Z)):
+        entries.append(tokens)
+    rows = jnp.concatenate(lax.all_to_all(jnp.stack(entries), Z, 0, 0), axis=0)
     near = lax.all_to_all(jnp.broadcast_to(rows, (2, *rows.shape)), "xh", 0, 0)
     rows = near.reshape(-1, tokens.shape[1])
     n_rows = rows.shape[0]

time: 148 us -> 173 us (1.17)
  waiting for transfers between devices: 21.9 us -> 59.2 us
  blocking collectives: 99.5 us -> 63.7 us
  starting transfers between devices: 16.6 us -> 35.4 us
  local copies, waits for them, and re-layouts: 3.77 us -> 6.37 us
    all_gather x1 -> x0, blocking collectives: 38.8 us -> none  [shards(): rows = lax.all_gather(tokens, Z, axis=0, tiled=True)]
    all_to_all x0 -> x2, waiting for transfers between devices: none -> 35.6 us  [the longest x1 24.7 us: shards(): rows = jnp.concatenate(lax.all_to_all(jnp.stack(entries), Z, 0, 0), axis=0)]
    all_to_all x0 -> x2, starting transfers between devices: none -> 18.8 us  [the longest x1 15.2 us: shards(): rows = jnp.concatenate(lax.all_to_all(jnp.stack(entries), Z, 0, 0), axis=0)]
    all_to_all x1 -> x0, blocking collectives: 14.2 us -> none  [shards(): near = lax.all_to_all(jnp.broadcast_to(rows, (2, *rows.shape)), 'xh', 0, 0)]
    all_to_all x1, blocking collectives: 23.7 us -> 36.7 us  [shards(): mixed = lax.all_to_all(mixed, ('zl', 'xh'), 0, 0)]
    all_to_all x1, blocking collectives: 22.8 us -> 27 us  [shards(): mixed = lax.all_to_all(mixed.reshape(4, 16, -1), 'zh', 0, 0)]
  transfers between devices with their start and end apart: 5 -> 7, of which waited for: 2 -> 4; matrix products, arithmetic and copies ran while one was open for 2% -> 3% of each run, Pallas kernels for 0% -> 0%
where the time goes in v1:
time: 173 us; the launch traced here: 172 us
  blocking collectives  63.7 us (37%)
  waiting for transfers between devices  59.2 us (34%)
  starting transfers between devices  35.4 us (20%)
  local copies, waits for them, and re-layouts  6.37 us (4%)
  matrix products  5.98 us (3%)
    all_to_all x1, blocking collectives, shards(): mixed = lax.all_to_all(mixed, ('zl', 'xh'), 0, 0)  36.7 us
    all_to_all x1, blocking collectives, shards(): mixed = lax.all_to_all(mixed.reshape(4, 16, -1), 'zh', 0, 0)  27 us
    all_to_all x1, waiting for transfers between devices, shards(): rows = jnp.concatenate(lax.all_to_all(jnp.stack(entries), Z, 0, 0), axis=0)  24.7 us
    all_to_all x1, starting transfers between devices, shards(): rows = jnp.concatenate(lax.all_to_all(jnp.stack(entries), Z, 0, 0), axis=0)  15.2 us
    all_to_all x1, waiting for transfers between devices, shards(): parts = lax.all_to_all(partial, NARROW, 0, 0)  13.1 us
    all_to_all x1, waiting for transfers between devices, shards(): near = lax.all_to_all(jnp.broadcast_to(rows, (2, *rows.shape)), 'xh', 0, 0)  10.9 us
    all_to_all x1, waiting for transfers between devices, shards(): lax.all_to_all(jnp.broadcast_to(hidden, (8, *hidden.shape)), NARROW, 0, 0)  10.6 us
    all_to_all x1, starting transfers between devices, shards(): parts = lax.all_to_all(partial, NARROW, 0, 0)  6.05 us
  transfers between devices with their start and end apart: 7, of which 4 were waited for; matrix products, arithmetic and copies ran while one was open for 3% of the time, Pallas kernels for 0%

profile of v1, /device:TPU:2, one launch (start us, length us, event | category | flops | bytes accessed | tf_op | source)
XLA Modules:
  0.0 172.0 jit_solution(11887927216656544281)
XLA Ops:
  0.0 1.6 stack.2
  1.6 15.2 %all-to-all-start = ((bf16[16,16,1024]{2,1,0:T(8,128)(2,1)}), bf16[16,16,1024]{2,1,0:T(8,128)(2,1)S(1)}, u32[]{:S(2)}, u32[]{:S(2)}) async-start(bf16[16,16,1024]{2,1,0:T(8,128)(2,1)} %stack.2), calls=%async_computation | async-start | bytes 1048576 | tf_op jit(solution)/shard_map/all_to_all | solution.py:23
  16.8 1.9 %collective-permute-start = (bf16[1024,448]{0,1:T(8,128)(2,1)}, bf16[1024,448]{0,1:T(8,128)(2,1)}, u32[]{:S(2)}, u32[]{:S(2)}) collective-permute-start(bf16[1024,448]{0,1:T(8,128)(2,1)} %param.5), channel_id=1, source_target_pairs={{0,8},{8,0},{1,9},{9,1},{2,10},{10,2},{3,11},{11,3},{4,12},{12,4},... | collective-permute-start | bytes 2752520 | tf_op jit(solution)/shard_map/ppermute | solution.py:17
  18.7 2.4 %collective-permute-start.1 = (bf16[1024,448]{0,1:T(8,128)(2,1)}, bf16[1024,448]{0,1:T(8,128)(2,1)S(1)}, u32[]{:S(2)}, u32[]{:S(2)}) collective-permute-start(bf16[1024,448]{0,1:T(8,128)(2,1)} %param.6), channel_id=1, source_target_pairs={{0,8},{8,0},{1,9},{9,1},{2,10},{10,2},{3,11},{11,3},{4,12},{12,4},... | collective-permute-start | bytes 2752520 | tf_op jit(solution)/shard_map/ppermute | solution.py:18
  21.2 24.7 %all-to-all-done = bf16[16,16,1024]{2,1,0:T(8,128)(2,1)S(1)} async-done(((bf16[16,16,1024]{2,1,0:T(8,128)(2,1)}), bf16[16,16,1024]{2,1,0:T(8,128)(2,1)S(1)}, u32[]{:S(2)}, u32[]{:S(2)}) %all-to-all-start) | async-done | bytes 524320 | tf_op jit(solution)/shard_map/all_to_all | solution.py:23
  45.9 1.1 broadcast_in_dim.6
  47.0 3.6 %all-to-all-start.1 = ((bf16[2,256,1024]{2,1,0:T(8,128)(2,1)}), bf16[2,256,1024]{2,1,0:T(8,128)(2,1)S(1)}, u32[]{:S(2)}, u32[]{:S(2)}) async-start(bf16[2,256,1024]{2,1,0:T(8,128)(2,1)} %broadcast_in_dim.6), calls=%async_computation.1 | async-start | bytes 2097152 | tf_op jit(solution)/shard_map/all_to_all | solution.py:24
  50.6 0.0 collective-permute-done
  50.6 10.9 %all-to-all-done.1 = bf16[2,256,1024]{2,1,0:T(8,128)(2,1)S(1)} async-done(((bf16[2,256,1024]{2,1,0:T(8,128)(2,1)}), bf16[2,256,1024]{2,1,0:T(8,128)(2,1)S(1)}, u32[]{:S(2)}, u32[]{:S(2)}) %all-to-all-start.1) | async-done | bytes 1048608 | tf_op jit(solution)/shard_map/all_to_all | solution.py:24
  61.5 0.0 copy-done
  61.5 2.4 %fusion.21 = bf16[512,896]{0,1:T(8,128)(2,1)S(1)} fusion(bf16[512,1024]{1,0:T(8,128)(2,1)S(1)} %bitcast.18, bf16[1024,448]{0,1:T(8,128)(2,1)} %collective-permute-done, bf16[1024,448]{0,1:T(8,128)(2,1)S(1)} %copy-done), kind=kOutput, calls=%fused_computation.17 | convolution fusion | flops 943652864 | bytes 3801088 | tf_op jit(solution)/shard_map/dot_general | solution.py:13
  63.9 0.0 collective-permute-done.1
  63.9 0.0 copy-done.1
  63.9 1.1 fusion.24
  65.1 0.1 pad_maximum_fusion
  65.2 2.5 %copy.7 = bf16[512,1792]{1,0:T(8,128)(2,1)} copy(bf16[512,1792]{0,1:T(8,128)(2,1)S(1)} %pad_maximum_fusion) | data formatting | bytes 3670016 | tf_op jit(solution)/shard_map/concatenate | solution.py:30
  67.7 6.1 %all-to-all-start.2 = ((bf16[8,64,1792]{2,1,0:T(8,128)(2,1)}), bf16[8,64,1792]{2,1,0:T(8,128)(2,1)S(1)}, u32[]{:S(2)}, u32[]{:S(2)}) async-start(bf16[8,64,1792]{2,1,0:T(8,128)(2,1)} %bitcast.4), calls=%async_computation.2 | async-start | bytes 3670016 | tf_op jit(solution)/shard_map/all_to_all | solution.py:34
  73.7 0.0 copy-done.2
  73.7 1.9 %collective-permute-start.2 = (bf16[448,1024]{1,0:T(8,128)(2,1)S(1)}, bf16[448,1024]{1,0:T(8,128)(2,1)}, u32[]{:S(2)}, u32[]{:S(2)}) collective-permute-start(bf16[448,1024]{1,0:T(8,128)(2,1)S(1)} %copy-done.2), channel_id=1, source_target_pairs={{0,8},{8,0},{1,9},{9,1},{2,10},{10,2},{3,11},{11,3},{4,12},{12,4},... | collective-permute-start | bytes 2752520 | tf_op jit(solution)/shard_map/ppermute | solution.py:19
  75.7 13.1 %all-to-all-done.2 = bf16[8,64,1792]{2,1,0:T(8,128)(2,1)S(1)} async-done(((bf16[8,64,1792]{2,1,0:T(8,128)(2,1)}), bf16[8,64,1792]{2,1,0:T(8,128)(2,1)S(1)}, u32[]{:S(2)}, u32[]{:S(2)}) %all-to-all-start.2) | async-done | bytes 1835040 | tf_op jit(solution)/shard_map/all_to_all | solution.py:34
  88.7 0.2 convert_reduce_fusion
  89.0 0.1 fusion.27
  89.0 1.1 broadcast_in_dim.7
  90.1 4.3 %all-to-all-start.3 = ((bf16[8,64,896]{2,1,0:T(8,128)(2,1)}), bf16[8,64,896]{2,1,0:T(8,128)(2,1)S(1)}, u32[]{:S(2)}, u32[]{:S(2)}) async-start(bf16[8,64,896]{2,1,0:T(8,128)(2,1)} %broadcast_in_dim.7), calls=%async_computation.3 | async-start | bytes 1835008 | tf_op jit(solution)/shard_map/all_to_all | solution.py:37
  94.4 0.0 collective-permute-done.2
  94.4 10.6 %all-to-all-done.3 = bf16[8,64,896]{2,1,0:T(8,128)(2,1)S(1)} async-done(((bf16[8,64,896]{2,1,0:T(8,128)(2,1)}), bf16[8,64,896]{2,1,0:T(8,128)(2,1)S(1)}, u32[]{:S(2)}, u32[]{:S(2)}) %all-to-all-start.3) | async-done | bytes 917536 | tf_op jit(solution)/shard_map/all_to_all | solution.py:37
  105.0 2.4 %fusion.12 = bf16[512,1024]{1,0:T(8,128)(2,1)S(1)} fusion(bf16[512,896]{1,0:T(8,128)(2,1)S(1)} %bitcast.21, bf16[448,1024]{1,0:T(8,128)(2,1)} %collective-permute-done.2, bf16[448,1024]{1,0:T(8,128)(2,1)S(1)} %copy-done.2), kind=kOutput, calls=%fused_computation.14 | convolution fusion | flops 943718400 | bytes 3801088 | tf_op jit(solution)/shard_map/dot_general | solution.py:13
  107.4 0.1 copy.8
  107.5 36.7 %all_to_all.30 = bf16[8,64,1024]{2,1,0:T(8,128)(2,1)S(1)} all-to-all(bf16[8,64,1024]{2,1,0:T(8,128)(2,1)S(1)} %bitcast.16), channel_id=1, replica_groups=mesh['zh'=4,'zl'=4,'xh'=2,'core'=2,'xl'=2,'y'=4] {'zl','xh'}, dimensions={0} | all-to-all | bytes 2097152 | tf_op jit(solution)/shard_map/all_to_all | solution.py:43
  144.2 0.2 reduce_sum.34
  144.4 27.0 %all_to_all.31 = bf16[4,16,1024]{2,1,0:T(8,128)(2,1)S(1)} all-to-all(bf16[4,16,1024]{2,1,0:T(8,128)(2,1)S(1)} %bitcast.22), channel_id=1, replica_groups=mesh['zh'=4,'zl'=4,'xh'=2,'core'=2,'xl'=2,'y'=4] {'zh'}, dimensions={0} | all-to-all | bytes 262144 | tf_op jit(solution)/shard_map/all_to_all | solution.py:45
  171.4 0.6 reduce_sum.35
  (3 shorter events, 0.0 us)
Async XLA Ops:
  1.6 44.3 %all-to-all-start = ((bf16[16,16,1024]{2,1,0:T(8,128)(2,1)}), bf16[16,16,1024]{2,1,0:T(8,128)(2,1)S(1)}, u32[]{:S(2)}, u32[]{:S(2)}) async-start(bf16[16,16,1024]{2,1,0:T(8,128)(2,1)} %stack.2), calls=%async_computation | async-start | bytes 1048576 | tf_op jit(solution)/shard_map/all_to_all | solution.py:23
  16.8 33.8 %collective-permute-start = (bf16[1024,448]{0,1:T(8,128)(2,1)}, bf16[1024,448]{0,1:T(8,128)(2,1)}, u32[]{:S(2)}, u32[]{:S(2)}) collective-permute-start(bf16[1024,448]{0,1:T(8,128)(2,1)} %param.5), channel_id=1, source_target_pairs={{0,8},{8,0},{1,9},{9,1},{2,10},{10,2},{3,11},{11,3},{4,12},{12,4},... | collective-permute-start | bytes 2752520 | tf_op jit(solution)/shard_map/ppermute | solution.py:17
  18.7 45.1 %collective-permute-start.1 = (bf16[1024,448]{0,1:T(8,128)(2,1)}, bf16[1024,448]{0,1:T(8,128)(2,1)S(1)}, u32[]{:S(2)}, u32[]{:S(2)}) collective-permute-start(bf16[1024,448]{0,1:T(8,128)(2,1)} %param.6), channel_id=1, source_target_pairs={{0,8},{8,0},{1,9},{9,1},{2,10},{10,2},{3,11},{11,3},{4,12},{12,4},... | collective-permute-start | bytes 2752520 | tf_op jit(solution)/shard_map/ppermute | solution.py:18
  45.9 15.6 %copy-start = (bf16[1024,448]{0,1:T(8,128)(2,1)S(1)}, bf16[1024,448]{0,1:T(8,128)(2,1)}, u32[]{:S(2)}) copy-start(bf16[1024,448]{0,1:T(8,128)(2,1)} %param.5) | copy-start | bytes 2752516
  47.0 14.5 %all-to-all-start.1 = ((bf16[2,256,1024]{2,1,0:T(8,128)(2,1)}), bf16[2,256,1024]{2,1,0:T(8,128)(2,1)S(1)}, u32[]{:S(2)}, u32[]{:S(2)}) async-start(bf16[2,256,1024]{2,1,0:T(8,128)(2,1)} %broadcast_in_dim.6), calls=%async_computation.1 | async-start | bytes 2097152 | tf_op jit(solution)/shard_map/all_to_all | solution.py:24
  61.5 2.4 %copy-start.1 = (bf16[1024,448]{0,1:T(8,128)(2,1)S(1)}, bf16[1024,448]{0,1:T(8,128)(2,1)}, u32[]{:S(2)}) copy-start(bf16[1024,448]{0,1:T(8,128)(2,1)} %param.6) | copy-start | bytes 2752516
  67.7 6.1 %copy-start.2 = (bf16[448,1024]{1,0:T(8,128)(2,1)S(1)}, bf16[448,1024]{1,0:T(8,128)(2,1)}, u32[]{:S(2)}) copy-start(bf16[448,1024]{1,0:T(8,128)(2,1)} %param.7) | copy-start | bytes 2752516
  67.7 21.0 %all-to-all-start.2 = ((bf16[8,64,1792]{2,1,0:T(8,128)(2,1)}), bf16[8,64,1792]{2,1,0:T(8,128)(2,1)S(1)}, u32[]{:S(2)}, u32[]{:S(2)}) async-start(bf16[8,64,1792]{2,1,0:T(8,128)(2,1)} %bitcast.4), calls=%async_computation.2 | async-start | bytes 3670016 | tf_op jit(solution)/shard_map/all_to_all | solution.py:34
  73.7 20.7 %collective-permute-start.2 = (bf16[448,1024]{1,0:T(8,128)(2,1)S(1)}, bf16[448,1024]{1,0:T(8,128)(2,1)}, u32[]{:S(2)}, u32[]{:S(2)}) collective-permute-start(bf16[448,1024]{1,0:T(8,128)(2,1)S(1)} %copy-done.2), channel_id=1, source_target_pairs={{0,8},{8,0},{1,9},{9,1},{2,10},{10,2},{3,11},{11,3},{4,12},{12,4},... | collective-permute-start | bytes 2752520 | tf_op jit(solution)/shard_map/ppermute | solution.py:19
  90.1 14.9 %all-to-all-start.3 = ((bf16[8,64,896]{2,1,0:T(8,128)(2,1)}), bf16[8,64,896]{2,1,0:T(8,128)(2,1)S(1)}, u32[]{:S(2)}, u32[]{:S(2)}) async-start(bf16[8,64,896]{2,1,0:T(8,128)(2,1)} %broadcast_in_dim.7), calls=%async_computation.3 | async-start | bytes 1835008 | tf_op jit(solution)/shard_map/all_to_all | solution.py:37
